TPU v7x, 32 devices: a whole 2x2x4 slice. The times are simulated.
32 devices in a mesh: grp: 2 (over y), gene: 4 (over z), cell: 4 (over x, core).
Axes of the slice: x: 2, y: 2, z: 4, core: 2. Of those that a mesh axis runs over, the one named last changes fastest.
Arguments:
- expression: bfloat16 [4096, 32768], P(('grp', 'cell'), 'gene'), parts along dimension 0, may hold values from -6 to 6
- gene_mask: int32 [4096, 32768], P(('grp', 'cell'), 'gene'), parts along dimension 0, may hold values 0 or 1
- mask_value: bfloat16 [32768], P('gene'), may hold values from -4 to 4
- w_qkv: bfloat16 [32768, 3072], P('gene'), may hold values from -0.03125 to 0.03125
- w_out: bfloat16 [1024, 32768], P(None, 'gene'), may hold values from -1.5 to 1.5
- w_first: bfloat16 [128, 256, 256], P('gene'), may hold values from -0.375 to 0.375
- w_second: bfloat16 [128, 256, 256], P('gene'), may hold values from -0.375 to 0.375
- cotangent: bfloat16 [4096, 32768], P(('grp', 'cell'), 'gene'), parts along dimension 0, may hold values from -6 to 6
Outputs:
- denoised: bfloat16 [4096, 32768], P(('grp', 'cell'), 'gene'), parts along dimension 0
- grad_first: float32 [256, 256, 256], P(('grp', 'gene'), 'cell'), parts along dimension 0
- grad_second: float32 [256, 256, 256], P(('grp', 'gene'), 'cell'), parts along dimension 0
There are 2 independent parts, one for each index of `grp`. A program takes and returns all parts, laid end to end along the dimension named above; an argument that names none is the same for every part. Nothing has to cross between parts.
All inputs are finite; a program needn't handle non-finite values. No bound on the sum of `gene_mask` on one device may be relied on, other than what follows from the above.
Results may differ from a plain program's by a relative error of at most 0.02.
Values may be sent and summed in bfloat16 or wider, within the bound.
A program may use at most 256 MiB of HBM per device.

v0:
```python
import jax
import jax.numpy as jnp
from jax import lax
from jax.sharding import PartitionSpec as P

HEADS = 16
HEAD_DIM = 64


def normalize(part):
    count = part.shape[0]
    shaped = part.reshape(count, HEADS, HEAD_DIM)
    meansq = jnp.mean(shaped * shaped, axis=-1, keepdims=True)
    return (
        (shaped * lax.rsqrt(meansq + 1e-06)).astype(jnp.bfloat16).reshape(count, HEADS * HEAD_DIM)
    )


def split_heads(qkv_sums):
    columns = qkv_sums.shape[1] // 3
    queries = normalize(qkv_sums[:, :columns])
    keys_normed = normalize(qkv_sums[:, columns : 2 * columns])
    values_b = qkv_sums[:, 2 * columns :].astype(jnp.bfloat16)
    return (queries, keys_normed, values_b)


def attend(queries, pieces):
    key_piece, value_piece = pieces
    query_count = queries.shape[0]
    key_count = key_piece.shape[0]
    query_heads = queries.reshape(query_count, HEADS, HEAD_DIM)
    key_heads = key_piece.reshape(key_count, HEADS, HEAD_DIM)
    value_heads = value_piece.reshape(key_count, HEADS, HEAD_DIM)
    scores = jnp.einsum(
        "qhd,khd->hqk", query_heads, key_heads, preferred_element_type=jnp.float32
    ) * HEAD_DIM ** (-0.5)
    expw = jnp.exp(scores).astype(jnp.bfloat16)
    denom = jnp.sum(expw, axis=2, dtype=jnp.float32)
    numer = jnp.einsum("hqk,khd->qhd", expw, value_heads, preferred_element_type=jnp.float32)
    return (numer, denom)


def finish(totals):
    numer, denom = totals
    query_count = numer.shape[0]
    return (numer / denom.T[:, :, None]).astype(jnp.bfloat16).reshape(query_count, HEADS * HEAD_DIM)


def on_device(expression, gene_mask, mask_value, w_qkv, w_out, w_first, w_second, cotangent):
    groups = lax.axis_size("gene")
    local_blocks = w_first.shape[0]
    block_size = w_first.shape[1]
    block_total = local_blocks * groups
    cell_rows = expression.shape[0]
    masked_in = jnp.where(gene_mask == 1, mask_value[None, :], expression)
    qkv_part = jnp.dot(masked_in, w_qkv, preferred_element_type=jnp.float32)
    qkv_full = lax.psum(qkv_part.astype(jnp.bfloat16), "gene").astype(jnp.float32)
    queries, keys_normed, values_b = split_heads(qkv_full)
    totals = attend(
        queries,
        (
            lax.all_gather(keys_normed, "cell", axis=0, tiled=True),
            lax.all_gather(values_b, "cell", axis=0, tiled=True),
        ),
    )
    attended = finish(totals)
    added = jnp.dot(attended, w_out, preferred_element_type=jnp.float32)
    hidden = (masked_in.astype(jnp.float32) + added).astype(jnp.bfloat16)
    blocks = hidden.reshape(cell_rows, local_blocks, block_size)
    first = jnp.einsum("cbi,bio->cbo", blocks, w_first, preferred_element_type=jnp.float32).astype(
        jnp.bfloat16
    )
    cot_blocks = cotangent.reshape(cell_rows, local_blocks, block_size)
    back_perm = jnp.einsum(
        "cjo,jko->cjk", cot_blocks, w_second, preferred_element_type=jnp.float32
    ).astype(jnp.bfloat16)
    back_send = back_perm.reshape(cell_rows, block_size // groups, block_total)
    received = lax.all_to_all(first, "gene", split_axis=2, concat_axis=1, tiled=True)
    permuted = jnp.swapaxes(received, 1, 2).reshape(cell_rows, local_blocks, block_size)
    mixed = jnp.einsum("cjk,jko->cjo", permuted, w_second, preferred_element_type=jnp.float32)
    denoised = (
        (blocks.astype(jnp.float32) + mixed)
        .astype(jnp.bfloat16)
        .reshape(cell_rows, local_blocks * block_size)
    )
    grad_second = jnp.einsum(
        "cjk,cjo->jko", permuted, cot_blocks, preferred_element_type=jnp.float32
    )
    back_recv = lax.all_to_all(back_send, "gene", split_axis=2, concat_axis=1, tiled=True)
    back_first = jnp.swapaxes(back_recv, 1, 2)
    grad_first = jnp.einsum("cbi,cbo->bio", blocks, back_first, preferred_element_type=jnp.float32)
    first_share, second_share = (
        lax.psum_scatter(
            grad_first.astype(jnp.bfloat16), "cell", scatter_dimension=1, tiled=True
        ).astype(jnp.float32),
        lax.psum_scatter(
            grad_second.astype(jnp.bfloat16), "cell", scatter_dimension=1, tiled=True
        ).astype(jnp.float32),
    )
    return (denoised, first_share, second_share)


def solution(mesh):
    placed = (
        P(("grp", "cell"), "gene"),
        P(("grp", "cell"), "gene"),
        P("gene"),
        P("gene", None),
        P(None, "gene"),
        P("gene", None, None),
        P("gene", None, None),
        P(("grp", "cell"), "gene"),
    )
    return jax.shard_map(
        on_device,
        mesh=mesh,
        in_specs=placed,
        out_specs=(
            P(("grp", "cell"), "gene"),
            P(("grp", "gene"), "cell", None),
            P(("grp", "gene"), "cell", None),
        ),
        check_vma=False,
    )
```

profile of v0, /device:TPU:0, one launch (start us, length us, event | category | flops | bytes accessed | tf_op | source)
XLA Modules:
  0.0 680.1 jit_solution(10328082861231233537)
XLA Ops:
  7.2 0.0 all-reduce.2.cloned.1.call-start
  7.2 9.0 %compare_select_fusion = bf16[512,8192]{1,0:T(8,128)(2,1)S(1)} fusion(bf16[512,8192]{1,0:T(8,128)(2,1)} %param.8, s32[512,8192]{1,0:T(8,128)} %param.9, bf16[8192]{0:T(1024)(128)(2,1)} %param.10), kind=kLoop, calls=%fused_computation.5 | loop fusion | flops 8388608 | bytes 33570816 | tf_op jit(solution)/shard_map/jit(_where)/select_n | solution.py:55
  16.3 3.4 copy-done
  19.7 32.1 %convolution_convert_fusion = bf16[512,3072]{1,0:T(8,128)(2,1)} fusion(bf16[512,8192]{1,0:T(8,128)(2,1)S(1)} %compare_select_fusion, bf16[8192,3072]{1,0:T(8,128)(2,1)} %param.11), kind=kOutput, calls=%fused_computation.16 | convolution fusion | flops 25771376640 | bytes 61865984 | tf_op jit(solution)/shard_map/dot_general | solution.py:56
  51.8 0.0 all-gather.5.cloned.1.call-start
  51.9 123.9 %all-reduce.2.cloned.1.call-done = bf16[512,3072]{1,0:T(8,128)(2,1)} async-done(((bf16[512,3072]{1,0:T(8,128)(2,1)}), bf16[512,3072]{1,0:T(8,128)(2,1)}) %all-reduce.2.cloned.1.call-update) | async-done | bytes 3145744 | tf_op jit(solution)/shard_map/psum | solution.py:57
  175.8 2.7 convert_element_type.61
  178.5 2.6 copy-done.1
  181.1 0.2 slice_multiply_fusion
  181.3 1.8 copy.61
  183.1 2.0 bitcast_reduce_fusion
  185.1 1.6 mul.39
  186.7 2.9 copy.62
  189.6 3.5 multiply_convert_fusion
  193.1 0.2 all-gather.3.cloned.1.call-start
  193.4 1.0 slice.13
  194.4 10.6 %fusion.9 = bf16[32,256,512]{2,1,0:T(8,128)(2,1)} fusion(bf16[32,256,256]{2,1,0:T(8,128)(2,1)} %param.14, bf16[64,32,8,256]{3,2,1,0:T(8,128)(2,1)} %bitcast.75), kind=kOutput, calls=%fused_computation.15 | convolution fusion | flops 2151677952 | bytes 20971520 | tf_op jit(solution)/shard_map/cjo,jko->cjk/dot_general | solution.py:74
  205.0 11.4 %copy.73 = bf16[512,64,128]{0,1,2:T(8,128)(2,1)} copy(bf16[512,64,128]{0,2,1:T(8,128)(2,1)} %bitcast.72) | data formatting | bytes 16777216 | tf_op jit(solution)/shard_map/reshape | solution.py:77
  216.4 5.8 all-to-all-start.1
  222.2 1.6 slice.14
  223.8 1.9 copy.60
  225.7 0.3 multiply_reduce_fusion
  226.1 0.7 all-gather.5.cloned.1.call-done
  226.8 6.5 copy.63
  233.3 30.1 %all-gather.3.cloned.1.call-done = bf16[2048,1024]{1,0:T(8,128)(2,1)} async-done(((bf16[512,1024]{1,0:T(8,128)(2,1)}), bf16[2048,1024]{1,0:T(8,128)(2,1)}) %all-gather.3.cloned.1.call-update) | async-done | bytes 4194320 | tf_op jit(solution)/shard_map/all_gather | solution.py:63
  263.4 6.5 copy.59
  269.9 18.0 %convert_reduce_fusion = (f32[16,512]{1,0:T(8,128)S(1)}, bf16[16,512,2048]{2,1,0:T(8,128)(2,1)}) fusion(bf16[2048,16,64]{0,2,1:T(8,128)(2,1)} %bitcast.79, f32[512,16,64]{0,2,1:T(8,128)S(1)} %bitcast.77, f32[512,16]{0,1:T(8,128)S(1)} %add_rsqrt_fusion.1), kind=kOutput, calls=%fused_computation | convolution fusion | flops 2215632896 | bytes 39911424 | tf_op jit(solution)/shard_map/qhd,khd->hqk/dot_general | solution.py:34
  287.9 17.0 %fusion.18 = bf16[512,16,64]{0,2,1:T(8,128)(2,1)S(1)} fusion(bf16[2048,16,64]{0,2,1:T(8,128)(2,1)} %bitcast.73, bf16[16,512,2048]{2,1,0:T(8,128)(2,1)} %get-tuple-element.16, f32[512,16]{0,1:T(8,128)S(1)} %bitcast.80), kind=kOutput, calls=%fused_computation.20 | convolution fusion | flops 2148532224 | bytes 38830080 | tf_op jit(solution)/shard_map/hqk,khd->qhd/dot_general | solution.py:39
  304.9 18.4 %add_convert_fusion = bf16[512,8192]{1,0:T(8,128)(2,1)} fusion(bf16[512,8192]{1,0:T(8,128)(2,1)} %copy-done, bf16[512,1024]{0,1:T(8,128)(2,1)S(1)} %bitcast.74, bf16[1024,8192]{1,0:T(8,128)(2,1)} %param.12), kind=kOutput, calls=%fused_computation.4 | convolution fusion | flops 8602517504 | bytes 34603008 | tf_op jit(solution)/shard_map/dot_general | solution.py:67
  323.3 12.0 %copy.84 = bf16[512,8192]{0,1:T(8,128)(2,1)} copy(bf16[512,8192]{1,0:T(8,128)(2,1)} %add_convert_fusion) | data formatting | bytes 16777216 | tf_op jit(solution)/shard_map/reshape | solution.py:69
  335.3 8.6 %convert_bitcast_fusion = bf16[512,32,256]{2,0,1:T(8,128)(2,1)} fusion(bf16[512,32,256]{0,2,1:T(8,128)(2,1)} %bitcast.64, bf16[32,256,256]{2,1,0:T(8,128)(2,1)} %param.13), kind=kOutput, calls=%fused_computation.12 | convolution fusion | flops 2151677952 | bytes 20971520 | tf_op jit(solution)/shard_map/cbi,bio->cbo/dot_general | solution.py:70
  343.9 14.7 %copy.66 = bf16[512,32,256]{0,1,2:T(8,128)(2,1)} copy(bf16[512,32,256]{2,0,1:T(8,128)(2,1)} %convert_bitcast_fusion) | data formatting | bytes 16777216 | tf_op jit(solution)/shard_map/convert_element_type | solution.py:70
  358.6 46.8 %all-to-all-done.1 = bf16[512,64,128]{0,1,2:T(8,128)(2,1)} async-done(((bf16[512,64,128]{0,1,2:T(8,128)(2,1)}), bf16[512,64,128]{0,1,2:T(8,128)(2,1)}, u32[]{:S(2)}, u32[]{:S(2)}) %all-to-all-start.1) | async-done | bytes 8388640 | tf_op jit(solution)/shard_map/all_to_all | solution.py:89
  405.4 5.6 all-to-all-start
  411.0 0.0 reduce-scatter.3.cloned.1.call-start
  411.1 11.6 %copy.75 = bf16[512,4,64,32]{0,3,2,1:T(8,128)(2,1)} copy(bf16[512,4,64,32]{0,2,3,1:T(8,128)(2,1)} %bitcast.21) | data formatting | bytes 16777216 | tf_op jit(solution)/shard_map/all_to_all | solution.py:89
  422.7 13.7 %copy.76 = bf16[512,256,32]{1,0,2:T(8,128)(2,1)} copy(bf16[512,256,32]{0,2,1:T(8,128)(2,1)} %bitcast.70) | data formatting | bytes 16777216 | tf_op jit(solution)/shard_map/all_to_all | solution.py:89
  436.4 10.2 %fusion.12 = bf16[32,256,256]{2,1,0:T(8,128)(2,1)} fusion(bf16[512,32,256]{0,2,1:T(8,128)(2,1)} %bitcast.65, bf16[512,256,32]{1,0,2:T(8,128)(2,1)} %copy.76), kind=kOutput, calls=%fused_computation.17 | convolution fusion | flops 2149580800 | bytes 20971520 | tf_op jit(solution)/shard_map/cbi,cbo->bio/dot_general | solution.py:91
  446.6 0.2 reduce-scatter.5.cloned.1.call-start
  446.8 146.8 %all-to-all-done = bf16[512,32,256]{0,1,2:T(8,128)(2,1)} async-done(((bf16[512,32,256]{0,1,2:T(8,128)(2,1)}), bf16[512,32,256]{0,1,2:T(8,128)(2,1)}, u32[]{:S(2)}, u32[]{:S(2)}) %all-to-all-start) | async-done | bytes 8388640 | tf_op jit(solution)/shard_map/all_to_all | solution.py:78
  593.6 11.6 %copy.68 = bf16[512,4,32,64]{0,3,2,1:T(8,128)(2,1)} copy(bf16[512,4,32,64]{0,2,3,1:T(8,128)(2,1)} %bitcast.11) | data formatting | bytes 16777216 | tf_op jit(solution)/shard_map/all_to_all | solution.py:78
  605.3 11.3 %copy.69 = bf16[512,64,128]{0,2,1:T(8,128)(2,1)} copy(bf16[512,64,128]{0,1,2:T(8,128)(2,1)} %bitcast.71) | data formatting | bytes 16777216 | tf_op jit(solution)/shard_map/transpose | solution.py:79
  616.6 10.3 %fusion.15 = bf16[32,256,256]{2,1,0:T(8,128)(2,1)} fusion(bf16[512,32,256]{0,2,1:T(8,128)(2,1)} %bitcast.67, bf16[64,32,8,256]{3,2,1,0:T(8,128)(2,1)} %bitcast.76), kind=kOutput, calls=%fused_computation.18 | convolution fusion | flops 2149580800 | bytes 20971520 | tf_op jit(solution)/shard_map/cjk,cjo->jko/dot_general | solution.py:86
  627.0 2.8 convert_element_type.75
  629.8 12.9 %fusion = bf16[512,32,256]{0,2,1:T(8,128)(2,1)} fusion(bf16[512,32,256]{0,2,1:T(8,128)(2,1)} %bitcast.66, bf16[512,32,256]{0,2,1:T(8,128)(2,1)} %bitcast.68, bf16[32,256,256]{2,1,0:T(8,128)(2,1)} %param.14), kind=kOutput, calls=%fused_computation.3 | convolution fusion | flops 2160066560 | bytes 29360128 | tf_op jit(solution)/shard_map/cjk,jko->cjo/dot_general | solution.py:80
  642.6 12.0 %copy.79 = bf16[512,8192]{1,0:T(8,128)(2,1)} copy(bf16[512,8192]{0,1:T(8,128)(2,1)} %bitcast.69) | data formatting | bytes 16777216
  654.6 16.0 %reduce-scatter.5.cloned.1.call-done = bf16[32,64,256]{2,1,0:T(8,128)(2,1)} async-done(((bf16[32,256,256]{2,1,0:T(8,128)(2,1)}), bf16[32,64,256]{2,1,0:T(8,128)(2,1)}) %reduce-scatter.5.cloned.1.call-update) | async-done | bytes 1048592 | tf_op jit(solution)/shard_map/reduce_scatter | solution.py:96
  670.6 2.8 convert_element_type.77
  (12 shorter events, 0.1 us)
Async XLA Ops:
  7.2 168.6 %all-reduce.2.cloned.1.call-start = ((), (), s32[]{:S(2)}) async-start(), calls=%async_computation.4 | async-start | bytes 6291456 | tf_op jit(solution)/shard_map/psum | solution.py:57
  16.3 3.4 copy-start
  51.8 175.0 %all-gather.5.cloned.1.call-start = ((), (), s32[]{:S(2)}) async-start(), calls=%async_computation.6 | async-start | bytes 5242880 | tf_op jit(solution)/shard_map/all_gather | solution.py:62
  178.4 2.7 copy-start.1
  183.1 10.3 %copy-start.2 = (bf16[512,3072]{1,0:T(8,128)(2,1)S(1)}, bf16[512,3072]{1,0:T(8,128)(2,1)}, u32[]{:S(2)}) copy-start(bf16[512,3072]{1,0:T(8,128)(2,1)} %all-reduce.2.cloned.1.call-done) | copy-start | bytes 9437188
  193.1 70.3 %all-gather.3.cloned.1.call-start = ((), (), s32[]{:S(2)}) async-start(), calls=%async_computation.5 | async-start | bytes 5242880 | tf_op jit(solution)/shard_map/all_gather | solution.py:63
  216.4 189.0 %all-to-all-start.1 = ((bf16[512,64,128]{0,1,2:T(8,128)(2,1)}), bf16[512,64,128]{0,1,2:T(8,128)(2,1)}, u32[]{:S(2)}, u32[]{:S(2)}) async-start(bf16[512,64,128]{0,1,2:T(8,128)(2,1)} %copy.73), calls=%async_computation.1 | async-start | bytes 16777216 | tf_op jit(solution)/shard_map/all_to_all | solution.py:89
  405.4 188.3 %all-to-all-start = ((bf16[512,32,256]{0,1,2:T(8,128)(2,1)}), bf16[512,32,256]{0,1,2:T(8,128)(2,1)}, u32[]{:S(2)}, u32[]{:S(2)}) async-start(bf16[512,32,256]{0,1,2:T(8,128)(2,1)} %copy.66), calls=%async_computation | async-start | bytes 16777216 | tf_op jit(solution)/shard_map/all_to_all | solution.py:78
  411.0 215.9 %reduce-scatter.3.cloned.1.call-start = ((), (), s32[]{:S(2)}) async-start(), calls=%async_computation.7 | async-start | bytes 5242880 | tf_op jit(solution)/shard_map/reduce_scatter | solution.py:93
  446.6 223.9 %reduce-scatter.5.cloned.1.call-start = ((), (), s32[]{:S(2)}) async-start(), calls=%async_computation.8 | async-start | bytes 5242880 | tf_op jit(solution)/shard_map/reduce_scatter | solution.py:96
Sparse Core Ops, SparseCore 0:
  51.9 123.7 all-reduce.1
  193.3 33.4 all-gather.4
  228.9 34.4 all-gather.2
  446.7 45.7 reduce-scatter.2
  627.0 43.4 reduce-scatter.4
where the time goes:
time: 688 us; the launch traced here: 680 us
  waiting for transfers between devices  364 us (53%)
  matrix products  138 us (20%)
  local copies, waits for them, and re-layouts  128 us (19%)
  other arithmetic  23.4 us (3%)
  between operations  14.1 us (2%)
  starting transfers between devices  12 us (2%)
    all_to_all x1, waiting for transfers between devices, on_device(): lax.all_to_all(first, 'gene', split_axis=2, concat_axis=1, tiled=True)  147 us
    psum x1, waiting for transfers between devices, on_device(): lax.psum(qkv_part.astype(jnp.bfloat16), 'gene').astype(jnp.float32)  124 us
    all_to_all x1, waiting for transfers between devices, on_device(): lax.all_to_all(back_send, 'gene', split_axis=2, concat_axis=1, tiled=True)  46.8 us
    dot_general x1, matrix products, on_device(): qkv_part = jnp.dot(masked_in, w_qkv, preferred_element_type=jnp.float32)  32.1 us
    all_gather x1, waiting for transfers between devices, on_device(): lax.all_gather(values_b, 'cell', axis=0, tiled=True)  30.1 us
    all_to_all x2, local copies, waits for them, and re-layouts, on_device(): lax.all_to_all(back_send, 'gene', split_axis=2, concat_axis=1, tiled=True)  25.3 us
    dot_general x1, matrix products, on_device(): added = jnp.dot(attended, w_out, preferred_element_type=jnp.float32)  18.4 us
    unnamed x7, local copies, waits for them, and re-layouts  18 us
  transfers between devices with their start and end apart: 7, of which 6 were waited for; matrix products, arithmetic and copies ran while one was open for 33% of the time, Pallas kernels for 0%

commit v1 on v0

--- a/solution.py
+++ b/solution.py
@@ -86,7 +86,12 @@
     grad_second = jnp.einsum(
         "cjk,cjo->jko", permuted, cot_blocks, preferred_element_type=jnp.float32
     )
-    back_recv = lax.all_to_all(back_send, "gene", split_axis=2, concat_axis=1, tiled=True)
+    back_recv = jnp.concatenate(
+        lax.all_to_all(
+            jnp.stack(jnp.split(back_send, lax.axis_size("gene"), axis=2)), "gene", 0, 0
+        ),
+        axis=1,
+    )
     back_first = jnp.swapaxes(back_recv, 1, 2)
     grad_first = jnp.einsum("cbi,cbo->bio", blocks, back_first, preferred_element_type=jnp.float32)
     first_share, second_share = (

time: 688 us -> 696 us (1.012)
  local copies, waits for them, and re-layouts: 128 us -> 109 us
  waiting for transfers between devices: 364 us -> 376 us
  starting transfers between devices: 12 us -> 22.7 us
    all_to_all x2 -> x0, local copies, waits for them, and re-layouts: 25.3 us -> none  [on_device(): lax.all_to_all(back_send, 'gene', split_axis=2, concat_axis=1, tiled=True)]
    all_to_all x1, waiting for transfers between devices: 147 us -> 159 us  [on_device(): lax.all_to_all(first, 'gene', split_axis=2, concat_axis=1, tiled=True)]
    all_to_all x1, starting transfers between devices: 5.84 us -> 16.7 us  [on_device(): lax.all_to_all(jnp.stack(jnp.split(back_send, lax.axis_size('gene'), axis...]
    all_to_all x1, waiting for transfers between devices: 46.8 us -> 54.5 us  [on_device(): lax.all_to_all(jnp.stack(jnp.split(back_send, lax.axis_size('gene'), axis...]
  transfers between devices with their start and end apart: 7 -> 7, of which waited for: 6 -> 5; matrix products, arithmetic and copies ran while one was open for 33% -> 31% of each run, Pallas kernels for 0% -> 0%
where the time goes in v1:
time: 696 us; the launch traced here: 686 us
  waiting for transfers between devices  376 us (54%)
  matrix products  138 us (20%)
  local copies, waits for them, and re-layouts  109 us (16%)
  other arithmetic  26.2 us (4%)
  starting transfers between devices  22.7 us (3%)
  between operations  14.4 us (2%)
    all_to_all x1, waiting for transfers between devices, on_device(): lax.all_to_all(first, 'gene', split_axis=2, concat_axis=1, tiled=True)  159 us
    psum x1, waiting for transfers between devices, on_device(): lax.psum(qkv_part.astype(jnp.bfloat16), 'gene').astype(jnp.float32)  124 us
    all_to_all x1, waiting for transfers between devices, on_device(): lax.all_to_all(jnp.stack(jnp.split(back_send, lax.axis_size('gene'), axis...  54.5 us
    dot_general x1, matrix products, on_device(): qkv_part = jnp.dot(masked_in, w_qkv, preferred_element_type=jnp.float32)  32.2 us
    all_gather x1, waiting for transfers between devices, on_device(): lax.all_gather(values_b, 'cell', axis=0, tiled=True)  23.4 us
    dot_general x1, matrix products, on_device(): added = jnp.dot(attended, w_out, preferred_element_type=jnp.float32)  18.4 us
    unnamed x7, local copies, waits for them, and re-layouts  18 us
    dot_general x1, matrix products, attend(): jnp.einsum('qhd,khd->hqk', query_heads, key_heads, preferred_element_type...  18 us
  transfers between devices with their start and end apart: 7, of which 5 were waited for; matrix products, arithmetic and copies ran while one was open for 31% of the time, Pallas kernels for 0%

profile of v1, /device:TPU:0, one launch (start us, length us, event | category | flops | bytes accessed | tf_op | source)
XLA Modules:
  0.0 686.1 jit_solution(11831191989982655681)
XLA Ops:
  7.2 0.0 all-reduce.2.cloned.1.call-start
  7.2 9.0 %compare_select_fusion = bf16[512,8192]{1,0:T(8,128)(2,1)S(1)} fusion(bf16[512,8192]{1,0:T(8,128)(2,1)} %param.8, s32[512,8192]{1,0:T(8,128)} %param.9, bf16[8192]{0:T(1024)(128)(2,1)} %param.10), kind=kLoop, calls=%fused_computation.5 | loop fusion | flops 8388608 | bytes 33570816 | tf_op jit(solution)/shard_map/jit(_where)/select_n | solution.py:55
  16.3 3.4 copy-done
  19.7 32.2 %convolution_convert_fusion = bf16[512,3072]{1,0:T(8,128)(2,1)} fusion(bf16[512,8192]{1,0:T(8,128)(2,1)S(1)} %compare_select_fusion, bf16[8192,3072]{1,0:T(8,128)(2,1)} %param.11), kind=kOutput, calls=%fused_computation.17 | convolution fusion | flops 25771376640 | bytes 61865984 | tf_op jit(solution)/shard_map/dot_general | solution.py:56
  51.9 0.0 all-gather.5.cloned.1.call-start
  51.9 123.9 %all-reduce.2.cloned.1.call-done = bf16[512,3072]{1,0:T(8,128)(2,1)} async-done(((bf16[512,3072]{1,0:T(8,128)(2,1)}), bf16[512,3072]{1,0:T(8,128)(2,1)}) %all-reduce.2.cloned.1.call-update) | async-done | bytes 3145744 | tf_op jit(solution)/shard_map/psum | solution.py:57
  175.8 2.7 convert_element_type.61
  178.5 2.7 copy-done.1
  181.1 1.6 slice_multiply_fusion
  182.7 1.9 copy.43
  184.7 0.3 bitcast_reduce_fusion
  185.0 1.6 mul.39
  186.6 1.9 copy.44
  188.5 2.9 multiply_convert_fusion
  191.4 0.0 all-gather.3.cloned.1.call-start
  191.4 10.6 %fusion.9 = bf16[32,256,512]{2,1,0:T(8,128)(2,1)} fusion(bf16[32,256,256]{2,1,0:T(8,128)(2,1)} %param.14, bf16[64,32,8,256]{3,2,1,0:T(8,128)(2,1)} %bitcast.81), kind=kOutput, calls=%fused_computation.16 | convolution fusion | flops 2151677952 | bytes 20971520 | tf_op jit(solution)/shard_map/cjo,jko->cjk/dot_general | solution.py:74
  202.1 1.0 slice.13
  203.1 4.1 slice_bitcast_fusion.3
  207.2 3.8 pad_maximum_fusion
  211.0 16.7 %all-to-all-start.1 = ((bf16[4,512,64,32]{1,3,2,0:T(8,128)(2,1)}), bf16[4,512,64,32]{1,3,2,0:T(8,128)(2,1)}, u32[]{:S(2)}, u32[]{:S(2)}) async-start(bf16[4,512,64,32]{1,3,2,0:T(8,128)(2,1)} %pad_maximum_fusion), calls=%async_computation.1 | async-start | bytes 16777216 | tf_op jit(solution)/shard_map/all_to_all | solution.py:90
  227.7 1.6 slice.14
  229.3 1.9 copy.42
  231.2 0.3 multiply_reduce_fusion
  231.6 0.0 all-gather.5.cloned.1.call-done
  231.6 6.7 copy.45
  238.3 23.4 %all-gather.3.cloned.1.call-done = bf16[2048,1024]{1,0:T(8,128)(2,1)} async-done(((bf16[512,1024]{1,0:T(8,128)(2,1)}), bf16[2048,1024]{1,0:T(8,128)(2,1)}) %all-gather.3.cloned.1.call-update) | async-done | bytes 4194320 | tf_op jit(solution)/shard_map/all_gather | solution.py:63
  261.7 6.5 copy.41
  268.2 18.0 %convert_reduce_fusion = (f32[16,512]{1,0:T(8,128)S(1)}, bf16[16,512,2048]{2,1,0:T(8,128)(2,1)}) fusion(bf16[2048,16,64]{0,2,1:T(8,128)(2,1)} %bitcast.85, f32[512,16,64]{0,2,1:T(8,128)S(1)} %bitcast.83, f32[512,16]{0,1:T(8,128)S(1)} %add_rsqrt_fusion.1), kind=kOutput, calls=%fused_computation | convolution fusion | flops 2215632896 | bytes 39911424 | tf_op jit(solution)/shard_map/qhd,khd->hqk/dot_general | solution.py:34
  286.1 17.0 %fusion.18 = bf16[512,16,64]{0,2,1:T(8,128)(2,1)S(1)} fusion(bf16[2048,16,64]{0,2,1:T(8,128)(2,1)} %bitcast.79, bf16[16,512,2048]{2,1,0:T(8,128)(2,1)} %get-tuple-element.17, f32[512,16]{0,1:T(8,128)S(1)} %bitcast.86), kind=kOutput, calls=%fused_computation.25 | convolution fusion | flops 2148532224 | bytes 38830080 | tf_op jit(solution)/shard_map/hqk,khd->qhd/dot_general | solution.py:39
  303.2 18.4 %add_convert_fusion = bf16[512,8192]{1,0:T(8,128)(2,1)} fusion(bf16[512,8192]{1,0:T(8,128)(2,1)} %copy-done, bf16[512,1024]{0,1:T(8,128)(2,1)S(1)} %bitcast.80, bf16[1024,8192]{1,0:T(8,128)(2,1)} %param.12), kind=kOutput, calls=%fused_computation.4 | convolution fusion | flops 8602517504 | bytes 34603008 | tf_op jit(solution)/shard_map/dot_general | solution.py:67
  321.6 12.0 %copy.62 = bf16[512,8192]{0,1:T(8,128)(2,1)} copy(bf16[512,8192]{1,0:T(8,128)(2,1)} %add_convert_fusion) | data formatting | bytes 16777216 | tf_op jit(solution)/shard_map/reshape | solution.py:69
  333.6 8.2 %convert_bitcast_fusion = bf16[512,32,256]{2,0,1:T(8,128)(2,1)} fusion(bf16[512,32,256]{0,2,1:T(8,128)(2,1)} %bitcast.71, bf16[32,256,256]{2,1,0:T(8,128)(2,1)} %param.13), kind=kOutput, calls=%fused_computation.13 | convolution fusion | flops 2151677952 | bytes 20971520 | tf_op jit(solution)/shard_map/cbi,bio->cbo/dot_general | solution.py:70
  341.8 14.7 %copy.48 = bf16[512,32,256]{0,1,2:T(8,128)(2,1)} copy(bf16[512,32,256]{2,0,1:T(8,128)(2,1)} %convert_bitcast_fusion) | data formatting | bytes 16777216 | tf_op jit(solution)/shard_map/convert_element_type | solution.py:70
  356.4 54.5 %all-to-all-done.1 = bf16[4,512,64,32]{1,3,2,0:T(8,128)(2,1)} async-done(((bf16[4,512,64,32]{1,3,2,0:T(8,128)(2,1)}), bf16[4,512,64,32]{1,3,2,0:T(8,128)(2,1)}, u32[]{:S(2)}, u32[]{:S(2)}) %all-to-all-start.1) | async-done | bytes 8388640 | tf_op jit(solution)/shard_map/all_to_all | solution.py:90
  410.9 5.7 all-to-all-start
  416.6 0.0 reduce-scatter.3.cloned.1.call-start
  416.6 13.7 %copy.55 = bf16[512,256,32]{1,0,2:T(8,128)(2,1)} copy(bf16[512,256,32]{0,2,1:T(8,128)(2,1)} %bitcast.25) | data formatting | bytes 16777216 | tf_op jit(solution)/shard_map/reshape | solution.py:89
  430.3 10.0 %fusion.12 = bf16[32,256,256]{2,1,0:T(8,128)(2,1)} fusion(bf16[512,32,256]{0,2,1:T(8,128)(2,1)} %bitcast.72, bf16[512,256,32]{1,0,2:T(8,128)(2,1)} %copy.55), kind=kOutput, calls=%fused_computation.18 | convolution fusion | flops 2149580800 | bytes 20971520 | tf_op jit(solution)/shard_map/cbi,cbo->bio/dot_general | solution.py:96
  440.4 0.2 reduce-scatter.5.cloned.1.call-start
  440.6 158.6 %all-to-all-done = bf16[512,32,256]{0,1,2:T(8,128)(2,1)} async-done(((bf16[512,32,256]{0,1,2:T(8,128)(2,1)}), bf16[512,32,256]{0,1,2:T(8,128)(2,1)}, u32[]{:S(2)}, u32[]{:S(2)}) %all-to-all-start) | async-done | bytes 8388640 | tf_op jit(solution)/shard_map/all_to_all | solution.py:78
  599.2 11.6 %copy.50 = bf16[512,4,32,64]{0,3,2,1:T(8,128)(2,1)} copy(bf16[512,4,32,64]{0,2,3,1:T(8,128)(2,1)} %bitcast.11) | data formatting | bytes 16777216 | tf_op jit(solution)/shard_map/all_to_all | solution.py:78
  610.8 11.3 %copy.51 = bf16[512,64,128]{0,2,1:T(8,128)(2,1)} copy(bf16[512,64,128]{0,1,2:T(8,128)(2,1)} %bitcast.78) | data formatting | bytes 16777216 | tf_op jit(solution)/shard_map/transpose | solution.py:79
  622.2 10.4 %fusion.15 = bf16[32,256,256]{2,1,0:T(8,128)(2,1)} fusion(bf16[512,32,256]{0,2,1:T(8,128)(2,1)} %bitcast.74, bf16[64,32,8,256]{3,2,1,0:T(8,128)(2,1)} %bitcast.82), kind=kOutput, calls=%fused_computation.19 | convolution fusion | flops 2149580800 | bytes 20971520 | tf_op jit(solution)/shard_map/cjk,cjo->jko/dot_general | solution.py:86
  632.6 2.8 convert_element_type.75
  635.4 13.0 %fusion = bf16[512,32,256]{0,2,1:T(8,128)(2,1)} fusion(bf16[512,32,256]{0,2,1:T(8,128)(2,1)} %bitcast.73, bf16[512,32,256]{0,2,1:T(8,128)(2,1)} %bitcast.75, bf16[32,256,256]{2,1,0:T(8,128)(2,1)} %param.14), kind=kOutput, calls=%fused_computation.3 | convolution fusion | flops 2160066560 | bytes 29360128 | tf_op jit(solution)/shard_map/cjk,jko->cjo/dot_general | solution.py:80
  648.4 12.0 %copy.58 = bf16[512,8192]{1,0:T(8,128)(2,1)} copy(bf16[512,8192]{0,1:T(8,128)(2,1)} %bitcast.76) | data formatting | bytes 16777216
  660.3 16.0 %reduce-scatter.5.cloned.1.call-done = bf16[32,64,256]{2,1,0:T(8,128)(2,1)} async-done(((bf16[32,256,256]{2,1,0:T(8,128)(2,1)}), bf16[32,64,256]{2,1,0:T(8,128)(2,1)}) %reduce-scatter.5.cloned.1.call-update) | async-done | bytes 1048592 | tf_op jit(solution)/shard_map/reduce_scatter | solution.py:101
  676.3 2.8 convert_element_type.77
  (12 shorter events, 0.1 us)
Async XLA Ops:
  7.2 168.6 %all-reduce.2.cloned.1.call-start = ((), (), s32[]{:S(2)}) async-start(), calls=%async_computation.4 | async-start | bytes 6291456 | tf_op jit(solution)/shard_map/psum | solution.py:57
  16.3 3.4 copy-start
  51.9 179.7 %all-gather.5.cloned.1.call-start = ((), (), s32[]{:S(2)}) async-start(), calls=%async_computation.6 | async-start | bytes 5242880 | tf_op jit(solution)/shard_map/all_gather | solution.py:62
  178.5 2.7 copy-start.1
  191.4 70.3 %all-gather.3.cloned.1.call-start = ((), (), s32[]{:S(2)}) async-start(), calls=%async_computation.5 | async-start | bytes 5242880 | tf_op jit(solution)/shard_map/all_gather | solution.py:63
  191.4 10.6 %copy-start.2 = (bf16[512,3072]{1,0:T(8,128)(2,1)S(1)}, bf16[512,3072]{1,0:T(8,128)(2,1)}, u32[]{:S(2)}) copy-start(bf16[512,3072]{1,0:T(8,128)(2,1)} %all-reduce.2.cloned.1.call-done) | copy-start | bytes 9437188
  211.0 199.9 %all-to-all-start.1 = ((bf16[4,512,64,32]{1,3,2,0:T(8,128)(2,1)}), bf16[4,512,64,32]{1,3,2,0:T(8,128)(2,1)}, u32[]{:S(2)}, u32[]{:S(2)}) async-start(bf16[4,512,64,32]{1,3,2,0:T(8,128)(2,1)} %pad_maximum_fusion), calls=%async_computation.1 | async-start | bytes 16777216 | tf_op jit(solution)/shard_map/all_to_all | solution.py:90
  410.9 188.3 %all-to-all-start = ((bf16[512,32,256]{0,1,2:T(8,128)(2,1)}), bf16[512,32,256]{0,1,2:T(8,128)(2,1)}, u32[]{:S(2)}, u32[]{:S(2)}) async-start(bf16[512,32,256]{0,1,2:T(8,128)(2,1)} %copy.48), calls=%async_computation | async-start | bytes 16777216 | tf_op jit(solution)/shard_map/all_to_all | solution.py:78
  416.6 216.0 %reduce-scatter.3.cloned.1.call-start = ((), (), s32[]{:S(2)}) async-start(), calls=%async_computation.7 | async-start | bytes 5242880 | tf_op jit(solution)/shard_map/reduce_scatter | solution.py:98
  440.4 235.9 %reduce-scatter.5.cloned.1.call-start = ((), (), s32[]{:S(2)}) async-start(), calls=%async_computation.8 | async-start | bytes 5242880 | tf_op jit(solution)/shard_map/reduce_scatter | solution.py:101
Sparse Core Ops, SparseCore 0:
  52.0 123.7 all-reduce.1
  191.5 33.4 all-gather.4
  227.2 34.4 all-gather.2
  440.5 45.8 reduce-scatter.2
  632.7 43.5 reduce-scatter.4
